TPU v7x, 32 devices: a whole 2x2x4 slice. The times are simulated.
32 devices in a mesh: grp: 4 (over y, x), pos: 8 (over z, core).
Axes of the slice: x: 2, y: 2, z: 4, core: 2. Of those that a mesh axis runs over, the one named last changes fastest.
Arguments:
- tiles: float32 [4, 8, 12, 256, 256], P('grp', 'pos'), may hold values from -0.109375 to 0.109375
- tile_row: int32 [4, 8, 12], P('grp', 'pos'), may hold values from 0 to 7
- tile_col: int32 [4, 8, 12], P('grp', 'pos'), may hold values from 0 to 7
- tile_count: int32 [4, 8], P('grp', 'pos'), may hold values from 1 to 12, as said below
- energies: float32 [16384], P('pos'), may hold values from 1 to 10
- basis: float32 [16, 16384], P(None, 'pos'), may hold values from -6 to 6
- prev_basis: float32 [16, 16384], P(None, 'pos'), may hold values from -6 to 6
- beta_prev: float32 [16, 16], replicated, may hold values from -3 to 3
Outputs:
- next_basis: float32 [16, 16384], P(None, 'pos')
- alpha: float32 [16, 16], replicated
- beta: float32 [16, 16], replicated
Inputs may be any that keep to these rules, and one draw needn't show every extreme that they name: `tile_count`: some segment of some diagonal uses all 12 slots in every draw.
All inputs are finite; a program needn't handle non-finite values.
Results may differ from a plain program's by a relative error of at most 0.00021.
Values sent between devices are 32-bit elements; how exact they have to be, the bound alone decides.
A program may use at most 64 MiB of HBM per device.

v0:
```python
import jax
import jax.numpy as jnp
from jax import lax
from jax.sharding import PartitionSpec as P


def passed_along(array, axis, by):
    peers = lax.axis_size(axis)
    return lax.ppermute(array, axis, [(i, (i + by) % peers) for i in range(peers)])


def matmul(left, right):
    return jnp.dot(left, right, precision=lax.Precision.HIGHEST)


def product(left, right):
    return jnp.dot(left, right.T, precision=lax.Precision.HIGHEST)


def rotate(values_in, offset):
    return passed_along(values_in, "pos", offset)


def shards(tiles, tile_row, tile_col, tile_count, energies, basis, prev_basis, beta_prev):
    slot_count = tiles.shape[2]
    tile_width = tiles.shape[-1]
    blocks = tiles.reshape(slot_count, tile_width, tile_width)
    vector_count, seg_len = basis.shape
    per_side = seg_len // tile_width
    highest = lax.Precision.HIGHEST
    live_mask = (jnp.arange(slot_count, dtype=jnp.int32) < tile_count.reshape(())).astype(
        jnp.float32
    )
    sides = jnp.arange(per_side, dtype=jnp.int32)
    row_hot = (tile_row.reshape(slot_count)[:, None] == sides[None, :]).astype(
        jnp.float32
    ) * live_mask[:, None]
    col_hot = (tile_col.reshape(slot_count)[:, None] == sides[None, :]).astype(
        jnp.float32
    ) * live_mask[:, None]
    own_rows = basis.reshape(vector_count, per_side, tile_width)
    group_index = lax.axis_index("grp")
    bit_count = lax.axis_size("grp").bit_length() - 1
    seg_total = lax.axis_size("pos")
    total_rows = float(seg_len * seg_total)

    def pick(level, arrived, kept):
        return jnp.where(group_index // (1 << level) % 2 == 1, arrived, kept)

    far_rows = own_rows
    for level in range(bit_count):
        far_rows = pick(level, rotate(far_rows, -(1 << level)), far_rows)
    picked = jnp.einsum("kt,btj->kbj", col_hot, far_rows, precision=highest)
    parts = jnp.einsum("kbj,kij->kbi", picked, blocks, precision=highest)
    forward = jnp.einsum("kt,kbi->bti", row_hot, parts, precision=highest)
    picked = jnp.einsum("kt,bti->kbi", row_hot, own_rows, precision=highest)
    parts = jnp.einsum("kbi,kij->kbj", picked, blocks, precision=highest)
    back_rows = jnp.einsum("kt,kbj->btj", col_hot, parts, precision=highest)
    for level in range(bit_count):
        back_rows = pick(level, rotate(back_rows, 1 << level), back_rows)
    partial_sum = (forward + back_rows).reshape(vector_count, seg_len)
    applied = lax.psum(partial_sum, "grp") + energies[None, :] * basis
    alpha = lax.psum(product(basis, applied), "pos") / total_rows
    residual = applied - matmul(alpha.T, basis) - matmul(beta_prev, prev_basis)
    gram = lax.psum(product(residual, residual), "pos") / total_rows
    factor = jnp.linalg.cholesky(gram)
    next_rows = jax.scipy.linalg.solve_triangular(factor, residual, lower=True)
    return (next_rows, alpha, factor)


def solution(mesh):
    in_specs = (
        P("grp", "pos", None, None, None),
        P("grp", "pos", None),
        P("grp", "pos", None),
        P("grp", "pos"),
        P("pos"),
        P(None, "pos"),
        P(None, "pos"),
        P(),
    )
    out_specs = (P(None, "pos"), P(), P())
    return jax.shard_map(shards, mesh=mesh, in_specs=in_specs, out_specs=out_specs, check_vma=False)
```

profile of v0, /device:TPU:0, one launch (start us, length us, event | category | flops | bytes accessed | tf_op | source)
XLA Modules:
  0.0 120.1 jit_solution(79853631742649549)
XLA Ops:
  7.2 0.0 copy-start
  7.2 0.0 copy-start.5
  7.2 0.0 all-reduce.2.cloned.1.call-start
  7.2 1.1 copy.19
  8.3 4.6 %collective-permute-start = (f32[16,8,256]{2,1,0:T(8,128)S(1)}, f32[16,8,256]{2,1,0:T(8,128)}, u32[]{:S(2)}, u32[]{:S(2)}) collective-permute-start(f32[16,8,256]{2,1,0:T(8,128)S(1)} %bitcast.48), channel_id=1, source_target_pairs={{0,7},{1,0},{2,1},{3,2},{4,3},{5,4},{6,5},{7,6},{8,15},{9,8},{10,9... | collective-permute-start | bytes 393224 | tf_op jit(solution)/shard_map/ppermute | solution.py:9
  13.6 1.1 fusion.15
  14.7 0.0 copy-done
  14.7 1.7 %fusion = f32[12,16,256]{2,1,0:T(8,128)S(1)} fusion(f32[1,1,12,256,256]{4,3,2,1,0:T(8,128)S(1)} %copy-done, f32[12,16,256]{2,0,1:T(8,128)S(1)} %fusion.15), kind=kOutput, calls=%fused_computation | convolution fusion | flops 150994944 | bytes 3538944 | tf_op jit(solution)/shard_map/kbi,kij->kbj/dot_general | solution.py:57
  16.4 0.0 copy-done.5
  16.4 0.4 convolution_bitcast_fusion
  16.8 0.0 copy-start.1
  16.8 0.0 copy-start.3
  16.8 0.1 collective-permute-start.2
  16.9 0.0 collective-permute-done
  17.0 1.1 collective-permute-start.1
  18.0 5.2 %collective-permute-done.2 = f32[16,8,256]{2,1,0:T(8,128)} collective-permute-done((f32[16,8,256]{2,1,0:T(8,128)S(1)}, f32[16,8,256]{2,1,0:T(8,128)}, u32[]{:S(2)}, u32[]{:S(2)}) %collective-permute-start.2) | collective-permute-done | bytes 131104 | tf_op jit(solution)/shard_map/ppermute | solution.py:9
  23.3 0.0 copy-start.2
  23.3 0.0 copy-start.4
  23.3 0.1 collective-permute-start.3
  23.4 0.0 collective-permute-done.1
  23.4 0.4 fusion.8
  23.8 2.8 %fusion.2 = f32[12,16,256]{2,1,0:T(8,128)S(1)} fusion(f32[1,1,12,256,256]{4,3,2,1,0:T(8,128)S(1)} %copy-done, f32[12,16,256]{2,0,1:T(8,128)S(1)} %fusion.8), kind=kOutput, calls=%fused_computation.2 | convolution fusion | flops 150994944 | bytes 3538944 | tf_op jit(solution)/shard_map/kbj,kij->kbi/dot_general | solution.py:54
  26.6 1.1 convolution_bitcast_fusion.1
  27.7 2.5 %collective-permute-done.3 = f32[16,8,256]{2,1,0:T(8,128)S(1)} collective-permute-done((f32[16,8,256]{2,1,0:T(8,128)S(1)}, f32[16,8,256]{2,1,0:T(8,128)S(1)}, u32[]{:S(2)}, u32[]{:S(2)}) %collective-permute-start.3) | collective-permute-done | bytes 131104 | tf_op jit(solution)/shard_map/ppermute | solution.py:9
  30.2 0.7 copy.20
  30.9 0.0 all-reduce.2.cloned.1.call-update
  30.9 42.9 %all-reduce.2.cloned.1.call-done = f32[16,2048]{1,0:T(8,128)} async-done(((f32[16,2048]{1,0:T(8,128)}), f32[16,2048]{1,0:T(8,128)}) %all-reduce.2.cloned.1.call-update) | async-done | bytes 131088 | tf_op jit(solution)/shard_map/psum | solution.py:62
  73.9 0.0 copy-done.1
  73.9 0.0 copy-done.3
  73.9 1.2 convolution_bitcast_fusion.2
  75.0 16.2 %psum.22 = f32[16,16]{0,1:T(8,128)S(1)} all-reduce(f32[16,16]{0,1:T(8,128)S(1)} %convolution_bitcast_fusion.2), channel_id=1, replica_groups=mesh['grp'=4,'pos'=8] {'pos'}, use_global_device_ids=true, to_apply=%region_1.2 | all-reduce | flops 256 | bytes 2048 | tf_op jit(solution)/shard_map/psum | solution.py:63
  91.2 0.7 copy.13
  91.9 1.2 convolution_subtract_fusion.1
  93.1 0.0 copy-done.2
  93.1 0.0 copy-done.4
  93.1 0.3 convolution_subtract_fusion
  93.4 0.2 fusion.40
  93.6 14.0 %psum.23 = f32[16,16]{0,1:T(8,128)S(1)} all-reduce(f32[16,16]{0,1:T(8,128)S(1)} %fusion.40), channel_id=1, replica_groups=mesh['grp'=4,'pos'=8] {'pos'}, use_global_device_ids=true, to_apply=%region_2.3 | all-reduce | flops 256 | bytes 2048 | tf_op jit(solution)/shard_map/psum | solution.py:65
  107.6 0.1 copy.12
  107.7 1.5 %cholesky.16 = f32[16,16]{1,0:T(8,128)S(1)} custom-call(f32[16,16]{1,0:T(8,128)S(1)} %fusion.14), custom_call_target="Cholesky" | custom-call | tf_op jit(solution)/shard_map/jit(cholesky)/cholesky | solution.py:66
  109.1 0.6 compare_reduce_fusion
  109.8 1.2 %select_bitcast_fusion = (f32[1,16,16]{2,1,0:T(8,128)S(1)}, f32[16,16]{1,0:T(8,128)}) fusion(f32[16,16]{1,0:T(8,128)S(1)} %cholesky.16, pred[]{:T(512)} %compare_reduce_fusion), kind=kLoop, calls=%fused_computation.25 | loop fusion | flops 1024 | bytes 3073 | tf_op jit(solution)/shard_map/jit(_solve_triangular)/triangular_solve | solution.py:67
  111.0 1.2 %custom-call.7 = f32[1,16,16]{1,2,0:T(8,128)S(1)} custom-call(f32[1,16,16]{2,1,0:T(8,128)S(1)} %get-tuple-element.6), custom_call_target="InvertDiagBlocksLowerTriangular" | custom-call | tf_op jit(solution)/shard_map/jit(_solve_triangular)/triangular_solve | solution.py:67
  112.3 1.0 fusion.12
  (8 shorter events, 0.1 us)
Async XLA Ops:
  7.2 7.5 %copy-start = (f32[1,1,12,256,256]{4,3,2,1,0:T(8,128)S(1)}, f32[1,1,12,256,256]{4,3,2,1,0:T(8,128)}, u32[]{:S(2)}) copy-start(f32[1,1,12,256,256]{4,3,2,1,0:T(8,128)} %param.8) | copy-start | bytes 9437188
  7.2 9.2 %copy-start.5 = (s32[1,1,12]{2,1,0:T(1,128)S(1)}, s32[1,1,12]{2,1,0:T(1,128)}, u32[]{:S(2)}) copy-start(s32[1,1,12]{2,1,0:T(1,128)} %param.10) | copy-start | bytes 148
  7.2 66.7 %all-reduce.2.cloned.1.call-start = ((), (), s32[]{:S(2)}) async-start(), calls=%async_computation | async-start | bytes 262144 | tf_op jit(solution)/shard_map/psum | solution.py:62
  8.3 8.6 %collective-permute-start = (f32[16,8,256]{2,1,0:T(8,128)S(1)}, f32[16,8,256]{2,1,0:T(8,128)}, u32[]{:S(2)}, u32[]{:S(2)}) collective-permute-start(f32[16,8,256]{2,1,0:T(8,128)S(1)} %bitcast.48), channel_id=1, source_target_pairs={{0,7},{1,0},{2,1},{3,2},{4,3},{5,4},{6,5},{7,6},{8,15},{9,8},{10,9... | collective-permute-start | bytes 393224 | tf_op jit(solution)/shard_map/ppermute | solution.py:9
  16.8 57.0 %copy-start.1 = (f32[16,2048]{1,0:T(8,128)S(1)}, f32[16,2048]{1,0:T(8,128)}, u32[]{:S(2)}) copy-start(f32[16,2048]{1,0:T(8,128)} %param.13) | copy-start | bytes 393220
  16.8 57.0 %copy-start.3 = (f32[2048]{0:T(1024)S(1)}, f32[2048]{0:T(1024)}, u32[]{:S(2)}) copy-start(f32[2048]{0:T(1024)} %param.12) | copy-start | bytes 24580
  16.8 6.5 %collective-permute-start.2 = (f32[16,8,256]{2,1,0:T(8,128)S(1)}, f32[16,8,256]{2,1,0:T(8,128)}, u32[]{:S(2)}, u32[]{:S(2)}) collective-permute-start(f32[16,8,256]{2,1,0:T(8,128)S(1)} %convolution_bitcast_fusion), channel_id=1, source_target_pairs={{0,1},{1,2},{2,3},{3,4},{4,5},{5,6},{6,7},{7,0},{8,9},{9,10},{10,1... | collective-permute-start | bytes 393224 | tf_op jit(solution)/shard_map/ppermute | solution.py:9
  17.0 6.4 %collective-permute-start.1 = (f32[16,8,256]{2,1,0:T(8,128)S(1)}, f32[16,8,256]{2,1,0:T(8,128)S(1)}, u32[]{:S(2)}, u32[]{:S(2)}) collective-permute-start(f32[16,8,256]{2,1,0:T(8,128)S(1)} %broadcast_select_fusion.1), channel_id=1, source_target_pairs={{0,6},{1,7},{2,0},{3,1},{4,2},{5,3},{6,4},{7,5},{8,14},{9,15},{10,... | collective-permute-start | bytes 393224 | tf_op jit(solution)/shard_map/ppermute | solution.py:9
  23.3 69.8 %copy-start.2 = (f32[16,2048]{1,0:T(8,128)S(1)}, f32[16,2048]{1,0:T(8,128)}, u32[]{:S(2)}) copy-start(f32[16,2048]{1,0:T(8,128)} %param.14) | copy-start | bytes 393220
  23.3 69.8 %copy-start.4 = (f32[16,16]{1,0:T(8,128)S(1)}, f32[16,16]{1,0:T(8,128)}, u32[]{:S(2)}) copy-start(f32[16,16]{1,0:T(8,128)} %param.15) | copy-start | bytes 3076
  23.3 6.8 %collective-permute-start.3 = (f32[16,8,256]{2,1,0:T(8,128)S(1)}, f32[16,8,256]{2,1,0:T(8,128)S(1)}, u32[]{:S(2)}, u32[]{:S(2)}) collective-permute-start(f32[16,8,256]{2,1,0:T(8,128)S(1)} %broadcast_select_fusion), channel_id=1, source_target_pairs={{0,2},{1,3},{2,4},{3,5},{4,6},{5,7},{6,0},{7,1},{8,10},{9,11},{10,... | collective-permute-start | bytes 393224 | tf_op jit(solution)/shard_map/ppermute | solution.py:9
Sparse Core Ops, SparseCore 0:
  31.0 42.7 all-reduce.1
where the time goes:
time: 120 us
  waiting for transfers between devices  50.7 us (42%)
  blocking collectives  30.2 us (25%)
  between operations  14.9 us (12%)
  matrix products  11.3 us (9%)
  starting transfers between devices  5.78 us (5%)
  other arithmetic  4.7 us (4%)
  local copies, waits for them, and re-layouts  2.58 us (2%)
    psum x1, waiting for transfers between devices, shards(): applied = lax.psum(partial_sum, 'grp') + energies[None, :] * basis  42.9 us
    psum x1, blocking collectives, shards(): alpha = lax.psum(product(basis, applied), 'pos') / total_rows  16.2 us
    psum x1, blocking collectives, shards(): gram = lax.psum(product(residual, residual), 'pos') / total_rows  14 us
    ppermute x4, waiting for transfers between devices, passed_along(): lax.ppermute(array, axis, [(i, (i + by) % peers) for i in range(peers)])  7.71 us
    ppermute x4, starting transfers between devices, passed_along(): lax.ppermute(array, axis, [(i, (i + by) % peers) for i in range(peers)])  5.74 us
    dot_general x1, matrix products, shards(): parts = jnp.einsum('kbj,kij->kbi', picked, blocks, precision=highest)  2.76 us
    unnamed x15, local copies, waits for them, and re-layouts  2.51 us
    another operation x2, other arithmetic, shards(): next_rows = jax.scipy.linalg.solve_triangular(factor, residual, lower=True)  2.47 us
  transfers between devices with their start and end apart: 5, of which 3 were waited for; matrix products, arithmetic and copies ran while one was open for 6% of the time, Pallas kernels for 0%

commit v1 on v0

v1 whole, which is shorter than its diff:
```python
import functools

import jax
import jax.numpy as jnp
from jax import lax
from jax.experimental import pallas as pl
from jax.experimental.pallas import tpu as pltpu
from jax.sharding import PartitionSpec as P

MESH = pl.DeviceIdType.MESH
NT = (((1,), (1,)), ((), ()))
NN = (((1,), (0,)), ((), ()))
f32 = jnp.float32
bf16 = jnp.bfloat16


def exact(left, right, dims):
    return lax.dot_general(
        left, right, dims, precision=lax.Precision.HIGHEST, preferred_element_type=f32
    )


def split(values):
    high = values.astype(bf16)
    return high, (values - high.astype(f32)).astype(bf16)


def factored(gram):
    n = gram.shape[0]
    wide = jnp.concatenate([gram, jnp.eye(n, dtype=f32)], axis=1)
    row_at = lax.broadcasted_iota(jnp.int32, (n, 1), 0)
    done = jnp.zeros((n, 2 * n), f32)
    for j in range(n):
        column = wide[:, j : j + 1]
        scale = lax.rsqrt(wide[j : j + 1, j : j + 1])
        pivot = wide[j : j + 1, :] * scale
        done = jnp.where(row_at == j, pivot, done)
        wide = wide - jnp.where(row_at > j, column * scale, 0.0) * pivot
    return done[:, :n], done[:, n:]


def kernel(
    groups, segs,
    tiles_hbm, row_hbm, col_hbm, count_hbm, energies_hbm, basis_hbm, prev_hbm, beta_prev_hbm,
    next_ref, alpha_ref, beta_ref,
    tiles, rows, cols, count, energies, own, far, prev, beta_prev,
    own_split, far_split, products, back, forth, arrived, gathered, offset, both, early, late,
    in_sem, tile_sem, far_sem, back_send, back_recv, forth_send, forth_recv,
    gather_send, gather_recv, early_send, early_recv, late_send, late_recv,
):
    g, p = lax.axis_index("grp"), lax.axis_index("pos")
    slots, width = tiles.shape[0], tiles.shape[-1]
    vectors, length = own.shape
    sides = length // width
    part = length // groups
    total = float(length * segs)

    def at(group, pos):
        return (lax.rem(group + groups, groups), lax.rem(pos + segs, segs))

    def send(src, dst, send_sem, recv_sem, to):
        return pltpu.make_async_remote_copy(
            src_ref=src, dst_ref=dst, send_sem=send_sem, recv_sem=recv_sem,
            device_id=to, device_id_type=MESH,
        )

    small = [
        pltpu.make_async_copy(src, dst, in_sem.at[i])
        for i, (src, dst) in enumerate([
            (basis_hbm, own), (prev_hbm, prev), (energies_hbm, energies),
            (beta_prev_hbm, beta_prev), (row_hbm, rows), (col_hbm, cols), (count_hbm, count),
        ])
    ]
    for copy in small:
        copy.start()

    def tile_copy(k):
        return pltpu.make_async_copy(tiles_hbm.at[k], tiles.at[k], tile_sem.at[k])

    for k in range(slots):
        tile_copy(k).start()

    barrier = pltpu.get_barrier_semaphore()
    greeted = 0
    for d in range(1, segs):
        pl.semaphore_signal(barrier, inc=1, device_id=at(g, p + d), device_id_type=MESH)
        greeted += 1
    for d in range(1, groups):
        pl.semaphore_signal(barrier, inc=1, device_id=at(g + d, p), device_id_type=MESH)
        source = lax.rem(g - d + groups, groups)
        pl.semaphore_signal(barrier, inc=1, device_id=at(source, p - source), device_id_type=MESH)
        greeted += 2

    for copy in small:
        copy.wait()

    def stack(ref, out):
        for t in range(sides):
            high, low = split(ref[:, t * width : (t + 1) * width])
            out[t] = jnp.concatenate([high, low], axis=0)

    def multiply(picked, k, dims):
        high, low = split(tiles[k])
        both_parts = lax.dot_general(picked, high, dims, preferred_element_type=f32)
        both_parts += lax.dot_general(picked, low, dims, preferred_element_type=f32)
        return both_parts[:vectors] + both_parts[vectors:]

    def scatter(index, out):
        for t in range(sides):
            value = jnp.zeros((vectors, width), f32)
            for k in range(slots):
                live = jnp.logical_and(index[0, k] == t, k < count[0, 0])
                value = value + products[k] * jnp.where(live, 1.0, 0.0).astype(f32)
            step = min(width, part)
            for c in range(0, width, step):
                lane = t * width + c
                out[lane // part, :, lane % part : lane % part + step] = value[:, c : c + step]

    stack(own, own_split)
    both[0:vectors] = own[...]
    both[vectors:] = prev[...]
    offset[...] = energies[...] * own[...] - exact(beta_prev[...], prev[...], NN)
    early[p] = exact(own[...], both[...], NT)

    pl.semaphore_wait(barrier, greeted)

    far_copy = send(basis_hbm, far, far_sem.at[0], far_sem.at[1], at(g, p - g))

    @pl.when(g != 0)
    def _():
        far_copy.start()

    @pl.when(g == 0)
    def _():
        far[...] = own[...]

    early_copies = [
        send(early.at[p], early.at[p], early_send.at[d], early_recv.at[d], at(g, p + d))
        for d in range(1, segs)
    ]
    for copy in early_copies:
        copy.start()

    def backward(k, carry):
        tile_copy(k).wait()
        products[k] = multiply(own_split[rows[0, k]], k, NN)
        return carry

    lax.fori_loop(0, slots, backward, 0)
    scatter(cols, back)

    back_copies = []
    for d in range(groups):
        h = lax.rem(g + d, groups)
        back_copies.append(
            send(back.at[h], arrived.at[d], back_send.at[d], back_recv.at[d], at(h, p + g))
        )
    for copy in back_copies[1:]:
        copy.start()

    @pl.when(g != 0)
    def _():
        back_copies[0].start()

    @pl.when(g == 0)
    def _():
        arrived[0] = back[g]

    @pl.when(g != 0)
    def _():
        far_copy.wait()

    stack(far, far_split)

    def forward(k, carry):
        products[k] = multiply(far_split[cols[0, k]], k, NT)
        return carry

    lax.fori_loop(0, slots, forward, 0)
    scatter(rows, forth)

    forth_copies = []
    for d in range(1, groups):
        h = lax.rem(g + d, groups)
        forth_copies.append(
            send(forth.at[h], arrived.at[groups + d - 1], forth_send.at[d], forth_recv.at[d], at(h, p))
        )
    for copy in forth_copies:
        copy.start()
    for copy in forth_copies + back_copies[1:]:
        copy.wait()

    @pl.when(g != 0)
    def _():
        back_copies[0].wait()

    mine = forth[g]
    for d in range(2 * groups - 1):
        mine = mine + arrived[d]
    gathered[g] = mine

    gather_copies = [
        send(gathered.at[g], gathered.at[g], gather_send.at[d], gather_recv.at[d], at(g + d, p))
        for d in range(1, groups)
    ]
    for copy in gather_copies:
        copy.start()
    for copy in gather_copies:
        copy.wait()

    for h in range(groups):
        lanes = slice(h * part, (h + 1) * part)
        both[vectors:, lanes] = gathered[h] + offset[:, lanes]
    late[p] = exact(both[vectors:], both[...], NT)

    late_copies = [
        send(late.at[p], late.at[p], late_send.at[d], late_recv.at[d], at(g, p + d))
        for d in range(1, segs)
    ]
    for copy in late_copies:
        copy.start()
    for copy in early_copies:
        copy.wait()
    before = early[0]
    for s in range(1, segs):
        before = before + early[s]
    basis_basis, basis_prev = before[:, :vectors], before[:, vectors:]
    shift = exact(beta_prev[...], basis_prev, NT)
    for copy in late_copies:
        copy.wait()
    after = late[0]
    for s in range(1, segs):
        after = after + late[s]
    rest_basis, rest_rest = after[:, :vectors], after[:, vectors:]

    alpha_t = (rest_basis + shift) / total
    alpha_ref[...] = alpha_t.T
    gram = (
        rest_rest
        + exact(exact(alpha_t, basis_basis, NN) - rest_basis, alpha_t, NT)
        - exact(alpha_t, rest_basis, NT)
    ) / total
    residual = both[vectors:] - exact(alpha_t, own[...], NN)
    upper, inverse = factored(gram)
    beta_ref[...] = upper.T
    next_ref[...] = exact(inverse, residual, NN)


def shards(groups, segs, tiles, tile_row, tile_col, tile_count, energies, basis, prev_basis, beta_prev):
    slots, width = tiles.shape[2], tiles.shape[-1]
    vectors, length = basis.shape
    sides, part = length // width, length // groups
    dma = pltpu.SemaphoreType.DMA
    block = (vectors, length)
    return pl.pallas_call(
        functools.partial(kernel, groups, segs),
        out_shape=(
            jax.ShapeDtypeStruct(block, f32),
            jax.ShapeDtypeStruct((vectors, vectors), f32),
            jax.ShapeDtypeStruct((vectors, vectors), f32),
        ),
        in_specs=[pl.BlockSpec(memory_space=pl.ANY)] * 8,
        out_specs=tuple(pl.BlockSpec(memory_space=pltpu.VMEM) for _ in range(3)),
        scratch_shapes=[
            pltpu.VMEM((slots, width, width), f32),
            pltpu.SMEM((1, slots), jnp.int32),
            pltpu.SMEM((1, slots), jnp.int32),
            pltpu.SMEM((1, 1), jnp.int32),
            pltpu.VMEM((1, length), f32),
            pltpu.VMEM(block, f32),
            pltpu.VMEM(block, f32),
            pltpu.VMEM(block, f32),
            pltpu.VMEM((vectors, vectors), f32),
            pltpu.VMEM((sides, 2 * vectors, width), bf16),
            pltpu.VMEM((sides, 2 * vectors, width), bf16),
            pltpu.VMEM((slots, vectors, width), f32),
            pltpu.VMEM((groups, vectors, part), f32),
            pltpu.VMEM((groups, vectors, part), f32),
            pltpu.VMEM((2 * groups - 1, vectors, part), f32),
            pltpu.VMEM((groups, vectors, part), f32),
            pltpu.VMEM(block, f32),
            pltpu.VMEM((2 * vectors, length), f32),
            pltpu.VMEM((segs, vectors, 2 * vectors), f32),
            pltpu.VMEM((segs, vectors, 2 * vectors), f32),
            dma((7,)), dma((slots,)), dma((2,)),
            dma((groups,)), dma((groups,)), dma((groups,)), dma((groups,)),
            dma((groups,)), dma((groups,)),
            dma((segs,)), dma((segs,)), dma((segs,)), dma((segs,)),
        ],
        compiler_params=pltpu.CompilerParams(collective_id=0, has_side_effects=True),
    )(
        tiles.reshape(slots, width, width),
        tile_row.reshape(1, slots),
        tile_col.reshape(1, slots),
        tile_count.reshape(1, 1),
        energies.reshape(1, length),
        basis,
        prev_basis,
        beta_prev,
    )


def solution(mesh):
    groups, segs = mesh.shape["grp"], mesh.shape["pos"]
    in_specs = (
        P("grp", "pos", None, None, None),
        P("grp", "pos", None),
        P("grp", "pos", None),
        P("grp", "pos"),
        P("pos"),
        P(None, "pos"),
        P(None, "pos"),
        P(),
    )
    out_specs = (P(None, "pos"), P(), P())
    return jax.shard_map(
        functools.partial(shards, groups, segs),
        mesh=mesh, in_specs=in_specs, out_specs=out_specs, check_vma=False,
    )
```

time: 120 us -> 36.8 us (0.31)
  waiting for transfers between devices: 50.7 us -> 0 us
  Pallas kernels: 0 us -> 31.2 us
  blocking collectives: 30.2 us -> 0 us
  between operations: 14.9 us -> 1.29 us
  matrix products: 11.3 us -> 0 us
  starting transfers between devices: 5.78 us -> 0 us
  other arithmetic: 4.7 us -> 0 us
  local copies, waits for them, and re-layouts: 2.58 us -> 4.16 us
    psum x1 -> x0, waiting for transfers between devices: 42.9 us -> none  [shards(): applied = lax.psum(partial_sum, 'grp') + energies[None, :] * basis]
    pallas_call x0 -> x1, Pallas kernels: none -> 31.2 us  [shards(): pl.pallas_call(functools.partial(kernel, groups, segs), out_shape=(jax.Sh...]
    psum x2 -> x0, blocking collectives: 30.2 us -> none  [the longest x1 16.2 us: shards(): alpha = lax.psum(product(basis, applied), 'pos') / total_rows]
    dot_general x10 -> x0, matrix products: 10.3 us -> none  [the longest x1 2.76 us: shards(): parts = jnp.einsum('kbj,kij->kbi', picked, blocks, precision=highest)]
    ppermute x4 -> x0, waiting for transfers between devices: 7.71 us -> none  [passed_along(): lax.ppermute(array, axis, [(i, (i + by) % peers) for i in range(peers)])]
    ppermute x4 -> x0, starting transfers between devices: 5.74 us -> none  [passed_along(): lax.ppermute(array, axis, [(i, (i + by) % peers) for i in range(peers)])]
    another operation x5 -> x0, other arithmetic: 4.6 us -> none  [the longest x2 2.47 us: shards(): next_rows = jax.scipy.linalg.solve_triangular(factor, residual, lower=True)]
    unnamed x15 -> x3, local copies, waits for them, and re-layouts: 2.51 us -> 4.16 us
  transfers between devices with their start and end apart: 5 -> 0, of which waited for: 3 -> 0; matrix products, arithmetic and copies ran while one was open for 6% -> 0% of each run, Pallas kernels for 0% -> 0%
where the time goes in v1:
time: 36.8 us; the launch traced here: 36.6 us
  Pallas kernels  31.2 us (85%)
  local copies, waits for them, and re-layouts  4.16 us (11%)
  between operations  1.29 us (4%)
    pallas_call x1, Pallas kernels, shards(): pl.pallas_call(functools.partial(kernel, groups, segs), out_shape=(jax.Sh...  31.2 us
    unnamed x3, local copies, waits for them, and re-layouts  4.16 us

profile of v1, /device:TPU:0, one launch (start us, length us, event | category | flops | bytes accessed | tf_op | source)
XLA Modules:
  0.0 36.6 jit_solution(3731960498794639372)
XLA Ops:
  1.3 31.2 %shard_map.103 = (f32[16,2048]{1,0:T(8,128)}, f32[16,16]{1,0:T(8,128)}, f32[16,16]{1,0:T(8,128)}) custom-call(f32[12,256,256]{2,1,0:T(8,128)} %bitcast.4, s32[1,12]{1,0:T(1,128)} %bitcast.6, s32[1,12]{1,0:T(1,128)} %bitcast.7, s32[1,1]{1,0:T(1,128)S(6)} %copy.14.count_hbm, f32[1,2048]{1,0:T(1,128)} %bitcast.5, f32[16,2048]{1,0:T(8,128)} %basis_hbm.1, ...), custom_call_target="tpu_custom_call" | custom-call | tf_op jit(solution)/shard_map/pallas_call | solution.py:255
  32.5 1.6 %copy.15 = f32[16,2048]{1,0:T(8,128)} copy(f32[16,2048]{1,0:T(8,128)} %get-tuple-element.6) | data formatting | bytes 262144
  34.0 1.3 %copy.16 = f32[16,16]{1,0:T(8,128)} copy(f32[16,16]{1,0:T(8,128)} %get-tuple-element.7) | data formatting | bytes 2048
  35.3 1.3 %copy.17 = f32[16,16]{1,0:T(8,128)} copy(f32[16,16]{1,0:T(8,128)} %get-tuple-element.8) | data formatting | bytes 2048

commit v2 on v1

--- a/solution.py
+++ b/solution.py
@@ -42,7 +42,7 @@
 def kernel(
     groups, segs,
     tiles_hbm, row_hbm, col_hbm, count_hbm, energies_hbm, basis_hbm, prev_hbm, beta_prev_hbm,
-    next_ref, alpha_ref, beta_ref,
+    rest_ref, sums_ref,
     tiles, rows, cols, count, energies, own, far, prev, beta_prev,
     own_split, far_split, products, back, forth, arrived, gathered, offset, both, early, late,
     in_sem, tile_sem, far_sem, back_send, back_recv, forth_send, forth_recv,
@@ -53,7 +53,6 @@
     vectors, length = own.shape
     sides = length // width
     part = length // groups
-    total = float(length * segs)
 
     def at(group, pos):
         return (lax.rem(group + groups, groups), lax.rem(pos + segs, segs))
@@ -224,23 +223,28 @@
     before = early[0]
     for s in range(1, segs):
         before = before + early[s]
-    basis_basis, basis_prev = before[:, :vectors], before[:, vectors:]
-    shift = exact(beta_prev[...], basis_prev, NT)
     for copy in late_copies:
         copy.wait()
     after = late[0]
     for s in range(1, segs):
         after = after + late[s]
-    rest_basis, rest_rest = after[:, :vectors], after[:, vectors:]
-
-    alpha_t = (rest_basis + shift) / total
+    sums_ref[0] = before
+    sums_ref[1] = after
+    rest_ref[...] = both[vectors:]
+
+
+def finish(total, rest_ref, basis_ref, sums_ref, beta_prev_ref, next_ref, alpha_ref, beta_ref):
+    vectors = basis_ref.shape[0]
+    basis_basis, basis_prev = sums_ref[0, :, :vectors], sums_ref[0, :, vectors:]
+    rest_basis, rest_rest = sums_ref[1, :, :vectors], sums_ref[1, :, vectors:]
+    alpha_t = (rest_basis + exact(beta_prev_ref[...], basis_prev, NT)) / total
     alpha_ref[...] = alpha_t.T
     gram = (
         rest_rest
         + exact(exact(alpha_t, basis_basis, NN) - rest_basis, alpha_t, NT)
         - exact(alpha_t, rest_basis, NT)
     ) / total
-    residual = both[vectors:] - exact(alpha_t, own[...], NN)
+    residual = rest_ref[...] - exact(alpha_t, basis_ref[...], NN)
     upper, inverse = factored(gram)
     beta_ref[...] = upper.T
     next_ref[...] = exact(inverse, residual, NN)
@@ -252,15 +256,15 @@
     sides, part = length // width, length // groups
     dma = pltpu.SemaphoreType.DMA
     block = (vectors, length)
-    return pl.pallas_call(
+    vmem = pl.BlockSpec(memory_space=pltpu.VMEM)
+    rest, sums = pl.pallas_call(
         functools.partial(kernel, groups, segs),
         out_shape=(
             jax.ShapeDtypeStruct(block, f32),
-            jax.ShapeDtypeStruct((vectors, vectors), f32),
-            jax.ShapeDtypeStruct((vectors, vectors), f32),
+            jax.ShapeDtypeStruct((2, vectors, 2 * vectors), f32),
         ),
-        in_specs=[pl.BlockSpec(memory_space=pl.ANY)] * 8,
-        out_specs=tuple(pl.BlockSpec(memory_space=pltpu.VMEM) for _ in range(3)),
+        in_specs=[pl.BlockSpec(memory_space=pltpu.HBM)] * 8,
+        out_specs=(vmem, vmem),
         scratch_shapes=[
             pltpu.VMEM((slots, width, width), f32),
             pltpu.SMEM((1, slots), jnp.int32),
@@ -298,6 +302,16 @@
         prev_basis,
         beta_prev,
     )
+    return pl.pallas_call(
+        functools.partial(finish, float(length * segs)),
+        out_shape=(
+            jax.ShapeDtypeStruct(block, f32),
+            jax.ShapeDtypeStruct((vectors, vectors), f32),
+            jax.ShapeDtypeStruct((vectors, vectors), f32),
+        ),
+        in_specs=[vmem] * 4,
+        out_specs=(vmem, vmem, vmem),
+    )(rest, basis, sums, beta_prev)
 
 
 def solution(mesh):

time: 36.8 us -> 34.2 us (0.929)
  local copies, waits for them, and re-layouts: 4.16 us -> 0 us
  Pallas kernels: 31.2 us -> 32.8 us
    unnamed x3 -> x0, local copies, waits for them, and re-layouts: 4.16 us -> none
    pallas_call x0 -> x1, Pallas kernels: none -> 4.04 us  [shards(): pl.pallas_call(functools.partial(finish, float(length * segs)), out_shape...]
    pallas_call x1, Pallas kernels: 31.2 us -> 28.8 us  [shards(): pl.pallas_call(functools.partial(kernel, groups, segs), out_shape=(jax.Sh...]
where the time goes in v2:
time: 34.2 us; the launch traced here: 34.1 us
  Pallas kernels  32.8 us (96%)
  between operations  1.29 us (4%)
    pallas_call x1, Pallas kernels, shards(): pl.pallas_call(functools.partial(kernel, groups, segs), out_shape=(jax.Sh...  28.8 us
    pallas_call x1, Pallas kernels, shards(): pl.pallas_call(functools.partial(finish, float(length * segs)), out_shape...  4.04 us

profile of v2, /device:TPU:0, one launch (start us, length us, event | category | flops | bytes accessed | tf_op | source)
XLA Modules:
  0.0 34.1 jit_solution(7645562359568204132)
XLA Ops:
  1.3 28.8 %shard_map.103 = (f32[16,2048]{1,0:T(8,128)}, f32[2,16,32]{2,1,0:T(8,128)}) custom-call(f32[12,256,256]{2,1,0:T(8,128)} %bitcast.4, s32[1,12]{1,0:T(1,128)} %bitcast.6, s32[1,12]{1,0:T(1,128)} %bitcast.7, s32[1,1]{1,0:T(1,128)S(6)} %copy.11.count_hbm, f32[1,2048]{1,0:T(1,128)} %bitcast.5, f32[16,2048]{1,0:T(8,128)} %basis_ref.1, f32[16,2048]{1,0:T(8,128)} %prev_hbm.1, ...), custom_call_target="tpu_custom_call" | custom-call | tf_op jit(solution)/shard_map/pallas_call | solution.py:260
  30.0 4.0 %shard_map.104 = (f32[16,2048]{1,0:T(8,128)}, f32[16,16]{1,0:T(8,128)}, f32[16,16]{1,0:T(8,128)}) custom-call(f32[16,2048]{1,0:T(8,128)} %get-tuple-element.5.rest_ref, f32[16,2048]{1,0:T(8,128)} %basis_ref.1, f32[2,16,32]{2,1,0:T(8,128)} %get-tuple-element.6.sums_ref, f32[16,16]{1,0:T(8,128)} %beta_prev_ref.1), custom_call_target="tpu_custom_call" | custom-call | tf_op jit(solution)/shard_map/pallas_call | solution.py:305

commit v3 on v2

--- a/solution.py
+++ b/solution.py
@@ -25,27 +25,40 @@
     return high, (values - high.astype(f32)).astype(bf16)
 
 
+def packed(values):
+    half = values.shape[0] // 2
+    return jnp.concatenate([values[:half], values[half:]], axis=1)
+
+
+def unpacked(values):
+    half = values.shape[1] // 2
+    return jnp.concatenate([values[:, :half], values[:, half:]], axis=0)
+
+
 def factored(gram):
     n = gram.shape[0]
     wide = jnp.concatenate([gram, jnp.eye(n, dtype=f32)], axis=1)
     row_at = lax.broadcasted_iota(jnp.int32, (n, 1), 0)
+    columns = [jnp.broadcast_to(gram[:, k : k + 1], (n, 2 * n)) for k in range(n)]
     done = jnp.zeros((n, 2 * n), f32)
     for j in range(n):
-        column = wide[:, j : j + 1]
-        scale = lax.rsqrt(wide[j : j + 1, j : j + 1])
-        pivot = wide[j : j + 1, :] * scale
-        done = jnp.where(row_at == j, pivot, done)
-        wide = wide - jnp.where(row_at > j, column * scale, 0.0) * pivot
+        corner = columns[j][j : j + 1]
+        inverse = 1.0 / corner
+        row = wide[j : j + 1]
+        done = jnp.where(row_at == j, row * lax.rsqrt(corner), done)
+        for k in range(j + 1, n):
+            columns[k] = columns[k] - columns[j] * (columns[k][j : j + 1] * inverse)
+        wide = wide - columns[j] * (row * inverse)
     return done[:, :n], done[:, n:]
 
 
 def kernel(
     groups, segs,
     tiles_hbm, row_hbm, col_hbm, count_hbm, energies_hbm, basis_hbm, prev_hbm, beta_prev_hbm,
-    rest_ref, sums_ref,
+    rest_hbm, sums_ref,
     tiles, rows, cols, count, energies, own, far, prev, beta_prev,
     own_split, far_split, products, back, forth, arrived, gathered, offset, both, early, late,
-    in_sem, tile_sem, far_sem, back_send, back_recv, forth_send, forth_recv,
+    in_sem, tile_sem, far_send, far_recv, back_send, back_recv, forth_send, forth_recv,
     gather_send, gather_recv, early_send, early_recv, late_send, late_recv,
 ):
     g, p = lax.axis_index("grp"), lax.axis_index("pos")
@@ -62,22 +75,6 @@
             src_ref=src, dst_ref=dst, send_sem=send_sem, recv_sem=recv_sem,
             device_id=to, device_id_type=MESH,
         )
-
-    small = [
-        pltpu.make_async_copy(src, dst, in_sem.at[i])
-        for i, (src, dst) in enumerate([
-            (basis_hbm, own), (prev_hbm, prev), (energies_hbm, energies),
-            (beta_prev_hbm, beta_prev), (row_hbm, rows), (col_hbm, cols), (count_hbm, count),
-        ])
-    ]
-    for copy in small:
-        copy.start()
-
-    def tile_copy(k):
-        return pltpu.make_async_copy(tiles_hbm.at[k], tiles.at[k], tile_sem.at[k])
-
-    for k in range(slots):
-        tile_copy(k).start()
 
     barrier = pltpu.get_barrier_semaphore()
     greeted = 0
@@ -88,10 +85,24 @@
         pl.semaphore_signal(barrier, inc=1, device_id=at(g + d, p), device_id_type=MESH)
         source = lax.rem(g - d + groups, groups)
         pl.semaphore_signal(barrier, inc=1, device_id=at(source, p - source), device_id_type=MESH)
-        greeted += 2
-
+        pl.semaphore_signal(barrier, inc=1, device_id=at(g + d, p + g), device_id_type=MESH)
+        greeted += 3
+
+    small = [
+        pltpu.make_async_copy(src, dst, in_sem.at[i])
+        for i, (src, dst) in enumerate([
+            (basis_hbm, own), (prev_hbm, prev), (energies_hbm, energies),
+            (beta_prev_hbm, beta_prev), (row_hbm, rows), (col_hbm, cols), (count_hbm, count),
+        ])
+    ]
     for copy in small:
-        copy.wait()
+        copy.start()
+
+    def tile_copy(k):
+        return pltpu.make_async_copy(tiles_hbm.at[k], tiles.at[k], tile_sem.at[k])
+
+    for k in range(slots):
+        tile_copy(k).start()
 
     def stack(ref, out):
         for t in range(sides):
@@ -115,23 +126,31 @@
                 lane = t * width + c
                 out[lane // part, :, lane % part : lane % part + step] = value[:, c : c + step]
 
+    pl.semaphore_wait(barrier, greeted)
+
+    lanes = pl.ds(pl.multiple_of(g * part, part), part)
+    far_copies = []
+    for d in range(groups):
+        other = lax.rem(g + d, groups)
+        far_copies.append(
+            send(
+                basis_hbm.at[:, lanes], far.at[:, lanes], far_send.at[d], far_recv.at[d],
+                at(other, p - other),
+            )
+        )
+        pl.when(other != 0)(far_copies[d].start)
+
+    for copy in small:
+        copy.wait()
+
+    @pl.when(g == 0)
+    def _():
+        far[...] = own[...]
+
     stack(own, own_split)
     both[0:vectors] = own[...]
     both[vectors:] = prev[...]
-    offset[...] = energies[...] * own[...] - exact(beta_prev[...], prev[...], NN)
-    early[p] = exact(own[...], both[...], NT)
-
-    pl.semaphore_wait(barrier, greeted)
-
-    far_copy = send(basis_hbm, far, far_sem.at[0], far_sem.at[1], at(g, p - g))
-
-    @pl.when(g != 0)
-    def _():
-        far_copy.start()
-
-    @pl.when(g == 0)
-    def _():
-        far[...] = own[...]
+    early[p] = packed(exact(own[...], both[...], NT))
 
     early_copies = [
         send(early.at[p], early.at[p], early_send.at[d], early_recv.at[d], at(g, p + d))
@@ -165,9 +184,12 @@
     def _():
         arrived[0] = back[g]
 
+    offset[...] = energies[...] * own[...] - exact(beta_prev[...], prev[...], NN)
+
     @pl.when(g != 0)
     def _():
-        far_copy.wait()
+        for copy in far_copies:
+            copy.wait_recv()
 
     stack(far, far_split)
 
@@ -187,11 +209,9 @@
     for copy in forth_copies:
         copy.start()
     for copy in forth_copies + back_copies[1:]:
-        copy.wait()
-
-    @pl.when(g != 0)
-    def _():
-        back_copies[0].wait()
+        copy.wait_recv()
+
+    pl.when(g != 0)(back_copies[0].wait_recv)
 
     mine = forth[g]
     for d in range(2 * groups - 1):
@@ -205,12 +225,12 @@
     for copy in gather_copies:
         copy.start()
     for copy in gather_copies:
-        copy.wait()
+        copy.wait_recv()
 
     for h in range(groups):
         lanes = slice(h * part, (h + 1) * part)
         both[vectors:, lanes] = gathered[h] + offset[:, lanes]
-    late[p] = exact(both[vectors:], both[...], NT)
+    late[p] = packed(exact(both[vectors:], both[...], NT))
 
     late_copies = [
         send(late.at[p], late.at[p], late_send.at[d], late_recv.at[d], at(g, p + d))
@@ -218,25 +238,41 @@
     ]
     for copy in late_copies:
         copy.start()
+    rest_copy = pltpu.make_async_copy(both.at[vectors:], rest_hbm, in_sem.at[0])
+    rest_copy.start()
     for copy in early_copies:
-        copy.wait()
+        copy.wait_recv()
     before = early[0]
     for s in range(1, segs):
         before = before + early[s]
+    for copy in early_copies + forth_copies + back_copies[1:] + gather_copies + late_copies:
+        copy.wait_send()
+    pl.when(g != 0)(back_copies[0].wait_send)
+    for d in range(groups):
+        pl.when(lax.rem(g + d, groups) != 0)(far_copies[d].wait_send)
     for copy in late_copies:
-        copy.wait()
+        copy.wait_recv()
     after = late[0]
     for s in range(1, segs):
         after = after + late[s]
     sums_ref[0] = before
     sums_ref[1] = after
-    rest_ref[...] = both[vectors:]
-
-
-def finish(total, rest_ref, basis_ref, sums_ref, beta_prev_ref, next_ref, alpha_ref, beta_ref):
-    vectors = basis_ref.shape[0]
-    basis_basis, basis_prev = sums_ref[0, :, :vectors], sums_ref[0, :, vectors:]
-    rest_basis, rest_rest = sums_ref[1, :, :vectors], sums_ref[1, :, vectors:]
+    rest_copy.wait()
+
+
+def finish(
+    total, rest_hbm, basis_hbm, sums_ref, beta_prev_ref, next_ref, alpha_ref, beta_ref, rest, basis, sem
+):
+    copies = [
+        pltpu.make_async_copy(rest_hbm, rest, sem.at[0]),
+        pltpu.make_async_copy(basis_hbm, basis, sem.at[1]),
+    ]
+    for copy in copies:
+        copy.start()
+    vectors = beta_prev_ref.shape[0]
+    before, after = unpacked(sums_ref[0]), unpacked(sums_ref[1])
+    basis_basis, basis_prev = before[:, :vectors], before[:, vectors:]
+    rest_basis, rest_rest = after[:, :vectors], after[:, vectors:]
     alpha_t = (rest_basis + exact(beta_prev_ref[...], basis_prev, NT)) / total
     alpha_ref[...] = alpha_t.T
     gram = (
@@ -244,9 +280,11 @@
         + exact(exact(alpha_t, basis_basis, NN) - rest_basis, alpha_t, NT)
         - exact(alpha_t, rest_basis, NT)
     ) / total
-    residual = rest_ref[...] - exact(alpha_t, basis_ref[...], NN)
     upper, inverse = factored(gram)
     beta_ref[...] = upper.T
+    for copy in copies:
+        copy.wait()
+    residual = rest[...] - exact(alpha_t, basis[...], NN)
     next_ref[...] = exact(inverse, residual, NN)
 
 
@@ -261,10 +299,10 @@
         functools.partial(kernel, groups, segs),
         out_shape=(
             jax.ShapeDtypeStruct(block, f32),
-            jax.ShapeDtypeStruct((2, vectors, 2 * vectors), f32),
+            jax.ShapeDtypeStruct((2, vectors // 2, 4 * vectors), f32),
         ),
         in_specs=[pl.BlockSpec(memory_space=pltpu.HBM)] * 8,
-        out_specs=(vmem, vmem),
+        out_specs=(pl.BlockSpec(memory_space=pltpu.HBM), vmem),
         scratch_shapes=[
             pltpu.VMEM((slots, width, width), f32),
             pltpu.SMEM((1, slots), jnp.int32),
@@ -284,9 +322,9 @@
             pltpu.VMEM((groups, vectors, part), f32),
             pltpu.VMEM(block, f32),
             pltpu.VMEM((2 * vectors, length), f32),
-            pltpu.VMEM((segs, vectors, 2 * vectors), f32),
-            pltpu.VMEM((segs, vectors, 2 * vectors), f32),
-            dma((7,)), dma((slots,)), dma((2,)),
+            pltpu.VMEM((segs, vectors // 2, 4 * vectors), f32),
+            pltpu.VMEM((segs, vectors // 2, 4 * vectors), f32),
+            dma((7,)), dma((slots,)), dma((groups,)), dma((groups,)),
             dma((groups,)), dma((groups,)), dma((groups,)), dma((groups,)),
             dma((groups,)), dma((groups,)),
             dma((segs,)), dma((segs,)), dma((segs,)), dma((segs,)),
@@ -309,8 +347,9 @@
             jax.ShapeDtypeStruct((vectors, vectors), f32),
             jax.ShapeDtypeStruct((vectors, vectors), f32),
         ),
-        in_specs=[vmem] * 4,
+        in_specs=[pl.BlockSpec(memory_space=pltpu.HBM)] * 2 + [vmem] * 2,
         out_specs=(vmem, vmem, vmem),
+        scratch_shapes=[pltpu.VMEM(block, f32), pltpu.VMEM(block, f32), dma((2,))],
     )(rest, basis, sums, beta_prev)
 
 

time: 34.2 us -> 31.8 us (0.930)
  Pallas kernels: 32.8 us -> 30.2 us
    pallas_call x1, Pallas kernels: 28.8 us -> 27.4 us  [shards(): pl.pallas_call(functools.partial(kernel, groups, segs), out_shape=(jax.Sh...]
    pallas_call x1, Pallas kernels: 4.04 us -> 2.8 us  [shards(): pl.pallas_call(functools.partial(finish, float(length * segs)), out_shape...]
where the time goes in v3:
time: 31.8 us; the launch traced here: 31.5 us
  Pallas kernels  30.2 us (95%)
  between operations  1.29 us (4%)
    pallas_call x1, Pallas kernels, shards(): pl.pallas_call(functools.partial(kernel, groups, segs), out_shape=(jax.Sh...  27.4 us
    pallas_call x1, Pallas kernels, shards(): pl.pallas_call(functools.partial(finish, float(length * segs)), out_shape...  2.8 us

profile of v3, /device:TPU:0, one launch (start us, length us, event | category | flops | bytes accessed | tf_op | source)
XLA Modules:
  0.0 31.5 jit_solution(9142522911155764780)
XLA Ops:
  1.3 27.4 %shard_map.103 = (f32[16,2048]{1,0:T(8,128)}, f32[2,8,64]{2,1,0:T(8,128)}) custom-call(f32[12,256,256]{2,1,0:T(8,128)} %bitcast.4, s32[1,12]{1,0:T(1,128)} %bitcast.6, s32[1,12]{1,0:T(1,128)} %bitcast.7, s32[1,1]{1,0:T(1,128)S(6)} %copy.11.count_hbm, f32[1,2048]{1,0:T(1,128)} %bitcast.5, f32[16,2048]{1,0:T(8,128)} %basis_hbm.3, f32[16,2048]{1,0:T(8,128)} %prev_hbm.1, ...), custom_call_target="tpu_custom_call" | custom-call | tf_op jit(solution)/shard_map/pallas_call | solution.py:298
  28.7 2.8 %shard_map.104 = (f32[16,2048]{1,0:T(8,128)}, f32[16,16]{1,0:T(8,128)}, f32[16,16]{1,0:T(8,128)}) custom-call(f32[16,2048]{1,0:T(8,128)} %get-tuple-element.5.rest_hbm, f32[16,2048]{1,0:T(8,128)} %basis_hbm.3, f32[2,8,64]{2,1,0:T(8,128)} %get-tuple-element.6.sums_ref, f32[16,16]{1,0:T(8,128)} %beta_prev_ref.1), custom_call_target="tpu_custom_call" | custom-call | tf_op jit(solution)/shard_map/pallas_call | solution.py:343

commit v4 on v3

--- a/solution.py
+++ b/solution.py
@@ -57,9 +57,9 @@
     tiles_hbm, row_hbm, col_hbm, count_hbm, energies_hbm, basis_hbm, prev_hbm, beta_prev_hbm,
     rest_hbm, sums_ref,
     tiles, rows, cols, count, energies, own, far, prev, beta_prev,
-    own_split, far_split, products, back, forth, arrived, gathered, offset, both, early, late,
+    own_split, far_split, products, back, forth, arrived, gathered, offset, both, pair, late,
     in_sem, tile_sem, far_send, far_recv, back_send, back_recv, forth_send, forth_recv,
-    gather_send, gather_recv, early_send, early_recv, late_send, late_recv,
+    gather_send, gather_recv, pair_sem, late_send, late_recv,
 ):
     g, p = lax.axis_index("grp"), lax.axis_index("pos")
     slots, width = tiles.shape[0], tiles.shape[-1]
@@ -126,6 +126,22 @@
                 lane = t * width + c
                 out[lane // part, :, lane % part : lane % part + step] = value[:, c : c + step]
 
+    for copy in small:
+        copy.wait()
+
+    @pl.when(g == 0)
+    def _():
+        far[...] = own[...]
+
+    stack(own, own_split)
+    def backward(k, carry):
+        tile_copy(k).wait()
+        products[k] = multiply(own_split[rows[0, k]], k, NN)
+        return carry
+
+    lax.fori_loop(0, slots, backward, 0)
+    scatter(cols, back)
+
     pl.semaphore_wait(barrier, greeted)
 
     lanes = pl.ds(pl.multiple_of(g * part, part), part)
@@ -140,33 +156,6 @@
         )
         pl.when(other != 0)(far_copies[d].start)
 
-    for copy in small:
-        copy.wait()
-
-    @pl.when(g == 0)
-    def _():
-        far[...] = own[...]
-
-    stack(own, own_split)
-    both[0:vectors] = own[...]
-    both[vectors:] = prev[...]
-    early[p] = packed(exact(own[...], both[...], NT))
-
-    early_copies = [
-        send(early.at[p], early.at[p], early_send.at[d], early_recv.at[d], at(g, p + d))
-        for d in range(1, segs)
-    ]
-    for copy in early_copies:
-        copy.start()
-
-    def backward(k, carry):
-        tile_copy(k).wait()
-        products[k] = multiply(own_split[rows[0, k]], k, NN)
-        return carry
-
-    lax.fori_loop(0, slots, backward, 0)
-    scatter(cols, back)
-
     back_copies = []
     for d in range(groups):
         h = lax.rem(g + d, groups)
@@ -184,6 +173,10 @@
     def _():
         arrived[0] = back[g]
 
+    both[0:vectors] = own[...]
+    both[vectors:] = prev[...]
+    pair_slot, chip = lax.rem(p, 2), p // 2
+    pair[pair_slot, :, : 4 * vectors] = packed(exact(own[...], both[...], NT))
     offset[...] = energies[...] * own[...] - exact(beta_prev[...], prev[...], NN)
 
     @pl.when(g != 0)
@@ -230,33 +223,34 @@
     for h in range(groups):
         lanes = slice(h * part, (h + 1) * part)
         both[vectors:, lanes] = gathered[h] + offset[:, lanes]
-    late[p] = packed(exact(both[vectors:], both[...], NT))
-
+    pair[pair_slot, :, 4 * vectors :] = packed(exact(both[vectors:], both[...], NT))
+
+    pair_copy = send(
+        pair.at[pair_slot], pair.at[pair_slot], pair_sem.at[0], pair_sem.at[1],
+        at(g, p + 1 - 2 * pair_slot),
+    )
+    pair_copy.start()
+    rest_copy = pltpu.make_async_copy(both.at[vectors:], rest_hbm, in_sem.at[0])
+    rest_copy.start()
+    pair_copy.wait_recv()
+    late[chip] = pair[0] + pair[1]
     late_copies = [
-        send(late.at[p], late.at[p], late_send.at[d], late_recv.at[d], at(g, p + d))
-        for d in range(1, segs)
+        send(late.at[chip], late.at[chip], late_send.at[d], late_recv.at[d], at(g, p + 2 * d))
+        for d in range(1, segs // 2)
     ]
     for copy in late_copies:
         copy.start()
-    rest_copy = pltpu.make_async_copy(both.at[vectors:], rest_hbm, in_sem.at[0])
-    rest_copy.start()
-    for copy in early_copies:
-        copy.wait_recv()
-    before = early[0]
-    for s in range(1, segs):
-        before = before + early[s]
-    for copy in early_copies + forth_copies + back_copies[1:] + gather_copies + late_copies:
+    for copy in forth_copies + back_copies[1:] + gather_copies + [pair_copy]:
         copy.wait_send()
     pl.when(g != 0)(back_copies[0].wait_send)
     for d in range(groups):
         pl.when(lax.rem(g + d, groups) != 0)(far_copies[d].wait_send)
     for copy in late_copies:
-        copy.wait_recv()
+        copy.wait()
     after = late[0]
-    for s in range(1, segs):
+    for s in range(1, segs // 2):
         after = after + late[s]
-    sums_ref[0] = before
-    sums_ref[1] = after
+    sums_ref[...] = after
     rest_copy.wait()
 
 
@@ -270,7 +264,8 @@
     for copy in copies:
         copy.start()
     vectors = beta_prev_ref.shape[0]
-    before, after = unpacked(sums_ref[0]), unpacked(sums_ref[1])
+    before = unpacked(sums_ref[:, : 4 * vectors])
+    after = unpacked(sums_ref[:, 4 * vectors :])
     basis_basis, basis_prev = before[:, :vectors], before[:, vectors:]
     rest_basis, rest_rest = after[:, :vectors], after[:, vectors:]
     alpha_t = (rest_basis + exact(beta_prev_ref[...], basis_prev, NT)) / total
@@ -299,7 +294,7 @@
         functools.partial(kernel, groups, segs),
         out_shape=(
             jax.ShapeDtypeStruct(block, f32),
-            jax.ShapeDtypeStruct((2, vectors // 2, 4 * vectors), f32),
+            jax.ShapeDtypeStruct((vectors // 2, 8 * vectors), f32),
         ),
         in_specs=[pl.BlockSpec(memory_space=pltpu.HBM)] * 8,
         out_specs=(pl.BlockSpec(memory_space=pltpu.HBM), vmem),
@@ -322,12 +317,12 @@
             pltpu.VMEM((groups, vectors, part), f32),
             pltpu.VMEM(block, f32),
             pltpu.VMEM((2 * vectors, length), f32),
-            pltpu.VMEM((segs, vectors // 2, 4 * vectors), f32),
-            pltpu.VMEM((segs, vectors // 2, 4 * vectors), f32),
+            pltpu.VMEM((2, vectors // 2, 8 * vectors), f32),
+            pltpu.VMEM((segs // 2, vectors // 2, 8 * vectors), f32),
             dma((7,)), dma((slots,)), dma((groups,)), dma((groups,)),
             dma((groups,)), dma((groups,)), dma((groups,)), dma((groups,)),
             dma((groups,)), dma((groups,)),
-            dma((segs,)), dma((segs,)), dma((segs,)), dma((segs,)),
+            dma((2,)), dma((segs // 2,)), dma((segs // 2,)),
         ],
         compiler_params=pltpu.CompilerParams(collective_id=0, has_side_effects=True),
     )(

time: 31.8 us -> 34.2 us (1.075)
  Pallas kernels: 30.2 us -> 32.6 us
    pallas_call x1, Pallas kernels: 27.4 us -> 29.7 us  [shards(): pl.pallas_call(functools.partial(kernel, groups, segs), out_shape=(jax.Sh...]
where the time goes in v4:
time: 34.2 us; the launch traced here: 33.9 us
  Pallas kernels  32.6 us (95%)
  between operations  1.29 us (4%)
    pallas_call x1, Pallas kernels, shards(): pl.pallas_call(functools.partial(kernel, groups, segs), out_shape=(jax.Sh...  29.7 us
    pallas_call x1, Pallas kernels, shards(): pl.pallas_call(functools.partial(finish, float(length * segs)), out_shape...  2.95 us

profile of v4, /device:TPU:0, one launch (start us, length us, event | category | flops | bytes accessed | tf_op | source)
XLA Modules:
  0.0 33.9 jit_solution(7478701957156945957)
XLA Ops:
  1.3 29.7 %shard_map.103 = (f32[16,2048]{1,0:T(8,128)}, f32[8,128]{1,0:T(8,128)}) custom-call(f32[12,256,256]{2,1,0:T(8,128)} %bitcast.4, s32[1,12]{1,0:T(1,128)} %bitcast.6, s32[1,12]{1,0:T(1,128)} %bitcast.7, s32[1,1]{1,0:T(1,128)S(6)} %copy.11.count_hbm, f32[1,2048]{1,0:T(1,128)} %bitcast.5, f32[16,2048]{1,0:T(8,128)} %basis_hbm.3, f32[16,2048]{1,0:T(8,128)} %prev_hbm.1, ...), custom_call_target="tpu_custom_call" | custom-call | tf_op jit(solution)/shard_map/pallas_call | solution.py:293
  31.0 2.9 %shard_map.104 = (f32[16,2048]{1,0:T(8,128)}, f32[16,16]{1,0:T(8,128)}, f32[16,16]{1,0:T(8,128)}) custom-call(f32[16,2048]{1,0:T(8,128)} %get-tuple-element.5.rest_hbm, f32[16,2048]{1,0:T(8,128)} %basis_hbm.3, f32[8,128]{1,0:T(8,128)} %get-tuple-element.6.sums_ref, f32[16,16]{1,0:T(8,128)} %beta_prev_ref.1), custom_call_target="tpu_custom_call" | custom-call | tf_op jit(solution)/shard_map/pallas_call | solution.py:338

commit v5 on v4

--- a/solution.py
+++ b/solution.py
@@ -57,8 +57,8 @@
     tiles_hbm, row_hbm, col_hbm, count_hbm, energies_hbm, basis_hbm, prev_hbm, beta_prev_hbm,
     rest_hbm, sums_ref,
     tiles, rows, cols, count, energies, own, far, prev, beta_prev,
-    own_split, far_split, products, back, forth, arrived, gathered, offset, both, pair, late,
-    in_sem, tile_sem, far_send, far_recv, back_send, back_recv, forth_send, forth_recv,
+    own_split, far_split, products, back, plane, forth, arrived, gathered, offset, both, pair, late,
+    in_sem, tile_sem, far_send, far_recv, plane_send, plane_recv, back_send, back_recv, forth_send, forth_recv,
     gather_send, gather_recv, pair_sem, late_send, late_recv,
 ):
     g, p = lax.axis_index("grp"), lax.axis_index("pos")
@@ -83,10 +83,8 @@
         greeted += 1
     for d in range(1, groups):
         pl.semaphore_signal(barrier, inc=1, device_id=at(g + d, p), device_id_type=MESH)
-        source = lax.rem(g - d + groups, groups)
-        pl.semaphore_signal(barrier, inc=1, device_id=at(source, p - source), device_id_type=MESH)
         pl.semaphore_signal(barrier, inc=1, device_id=at(g + d, p + g), device_id_type=MESH)
-        greeted += 3
+        greeted += 2
 
     small = [
         pltpu.make_async_copy(src, dst, in_sem.at[i])
@@ -156,22 +154,35 @@
         )
         pl.when(other != 0)(far_copies[d].start)
 
+    plane_copies = []
+    for d in range(1, groups):
+        h = lax.rem(g + d, groups)
+        plane_copies.append(
+            send(back.at[h], plane.at[d - 1], plane_send.at[d], plane_recv.at[d], at(h, p))
+        )
+    for copy in plane_copies:
+        copy.start()
+
     back_copies = []
     for d in range(groups):
-        h = lax.rem(g + d, groups)
+        diagonal = lax.rem(g - d + groups, groups)
+        held = plane.at[d - 1] if d else back.at[g]
         back_copies.append(
-            send(back.at[h], arrived.at[d], back_send.at[d], back_recv.at[d], at(h, p + g))
-        )
-    for copy in back_copies[1:]:
-        copy.start()
-
-    @pl.when(g != 0)
-    def _():
-        back_copies[0].start()
-
-    @pl.when(g == 0)
-    def _():
-        arrived[0] = back[g]
+            (
+                diagonal != 0, held,
+                send(held, arrived.at[d], back_send.at[d], back_recv.at[d], at(g, p + diagonal)),
+            )
+        )
+
+    def passed_on(d):
+        remote, held, copy = back_copies[d]
+        pl.when(remote)(copy.start)
+
+        @pl.when(jnp.logical_not(remote))
+        def _():
+            arrived[d] = held[...]
+
+    passed_on(0)
 
     both[0:vectors] = own[...]
     both[vectors:] = prev[...]
@@ -179,6 +190,10 @@
     pair[pair_slot, :, : 4 * vectors] = packed(exact(own[...], both[...], NT))
     offset[...] = energies[...] * own[...] - exact(beta_prev[...], prev[...], NN)
 
+    for d in range(1, groups):
+        plane_copies[d - 1].wait_recv()
+        passed_on(d)
+
     @pl.when(g != 0)
     def _():
         for copy in far_copies:
@@ -201,10 +216,10 @@
         )
     for copy in forth_copies:
         copy.start()
-    for copy in forth_copies + back_copies[1:]:
+    for remote, held, copy in back_copies:
+        pl.when(remote)(copy.wait_recv)
+    for copy in forth_copies:
         copy.wait_recv()
-
-    pl.when(g != 0)(back_copies[0].wait_recv)
 
     mine = forth[g]
     for d in range(2 * groups - 1):
@@ -240,9 +255,10 @@
     ]
     for copy in late_copies:
         copy.start()
-    for copy in forth_copies + back_copies[1:] + gather_copies + [pair_copy]:
+    for copy in plane_copies + forth_copies + gather_copies + [pair_copy]:
         copy.wait_send()
-    pl.when(g != 0)(back_copies[0].wait_send)
+    for remote, held, copy in back_copies:
+        pl.when(remote)(copy.wait_send)
     for d in range(groups):
         pl.when(lax.rem(g + d, groups) != 0)(far_copies[d].wait_send)
     for copy in late_copies:
@@ -312,6 +328,7 @@
             pltpu.VMEM((sides, 2 * vectors, width), bf16),
             pltpu.VMEM((slots, vectors, width), f32),
             pltpu.VMEM((groups, vectors, part), f32),
+            pltpu.VMEM((groups - 1, vectors, part), f32),
             pltpu.VMEM((groups, vectors, part), f32),
             pltpu.VMEM((2 * groups - 1, vectors, part), f32),
             pltpu.VMEM((groups, vectors, part), f32),
@@ -321,7 +338,7 @@
             pltpu.VMEM((segs // 2, vectors // 2, 8 * vectors), f32),
             dma((7,)), dma((slots,)), dma((groups,)), dma((groups,)),
             dma((groups,)), dma((groups,)), dma((groups,)), dma((groups,)),
-            dma((groups,)), dma((groups,)),
+            dma((groups,)), dma((groups,)), dma((groups,)), dma((groups,)),
             dma((2,)), dma((segs // 2,)), dma((segs // 2,)),
         ],
         compiler_params=pltpu.CompilerParams(collective_id=0, has_side_effects=True),

time: 34.2 us -> 31.6 us (0.924)
  Pallas kernels: 32.6 us -> 30.1 us
    pallas_call x1, Pallas kernels: 29.7 us -> 27.1 us  [shards(): pl.pallas_call(functools.partial(kernel, groups, segs), out_shape=(jax.Sh...]
where the time goes in v5:
time: 31.6 us; the launch traced here: 31.4 us
  Pallas kernels  30.1 us (95%)
  between operations  1.29 us (4%)
    pallas_call x1, Pallas kernels, shards(): pl.pallas_call(functools.partial(kernel, groups, segs), out_shape=(jax.Sh...  27.1 us
    pallas_call x1, Pallas kernels, shards(): pl.pallas_call(functools.partial(finish, float(length * segs)), out_shape...  2.95 us

profile of v5, /device:TPU:0, one launch (start us, length us, event | category | flops | bytes accessed | tf_op | source)
XLA Modules:
  0.0 31.4 jit_solution(1918164637039275799)
XLA Ops:
  1.3 27.1 %shard_map.103 = (f32[16,2048]{1,0:T(8,128)}, f32[8,128]{1,0:T(8,128)}) custom-call(f32[12,256,256]{2,1,0:T(8,128)} %bitcast.4, s32[1,12]{1,0:T(1,128)} %bitcast.6, s32[1,12]{1,0:T(1,128)} %bitcast.7, s32[1,1]{1,0:T(1,128)S(6)} %copy.11.count_hbm, f32[1,2048]{1,0:T(1,128)} %bitcast.5, f32[16,2048]{1,0:T(8,128)} %basis_hbm.3, f32[16,2048]{1,0:T(8,128)} %prev_hbm.1, ...), custom_call_target="tpu_custom_call" | custom-call | tf_op jit(solution)/shard_map/pallas_call | solution.py:309
  28.4 2.9 %shard_map.104 = (f32[16,2048]{1,0:T(8,128)}, f32[16,16]{1,0:T(8,128)}, f32[16,16]{1,0:T(8,128)}) custom-call(f32[16,2048]{1,0:T(8,128)} %get-tuple-element.5.rest_hbm, f32[16,2048]{1,0:T(8,128)} %basis_hbm.3, f32[8,128]{1,0:T(8,128)} %get-tuple-element.6.sums_ref, f32[16,16]{1,0:T(8,128)} %beta_prev_ref.1), custom_call_target="tpu_custom_call" | custom-call | tf_op jit(solution)/shard_map/pallas_call | solution.py:355

commit v6 on v4

--- a/solution.py
+++ b/solution.py
@@ -126,22 +126,6 @@
                 lane = t * width + c
                 out[lane // part, :, lane % part : lane % part + step] = value[:, c : c + step]
 
-    for copy in small:
-        copy.wait()
-
-    @pl.when(g == 0)
-    def _():
-        far[...] = own[...]
-
-    stack(own, own_split)
-    def backward(k, carry):
-        tile_copy(k).wait()
-        products[k] = multiply(own_split[rows[0, k]], k, NN)
-        return carry
-
-    lax.fori_loop(0, slots, backward, 0)
-    scatter(cols, back)
-
     pl.semaphore_wait(barrier, greeted)
 
     lanes = pl.ds(pl.multiple_of(g * part, part), part)
@@ -155,6 +139,22 @@
             )
         )
         pl.when(other != 0)(far_copies[d].start)
+
+    for copy in small:
+        copy.wait()
+
+    @pl.when(g == 0)
+    def _():
+        far[...] = own[...]
+
+    stack(own, own_split)
+    def backward(k, carry):
+        tile_copy(k).wait()
+        products[k] = multiply(own_split[rows[0, k]], k, NN)
+        return carry
+
+    lax.fori_loop(0, slots, backward, 0)
+    scatter(cols, back)
 
     back_copies = []
     for d in range(groups):

time: 34.2 us -> 31.5 us (0.921)
  Pallas kernels: 32.6 us -> 30 us
    pallas_call x1, Pallas kernels: 29.7 us -> 27 us  [shards(): pl.pallas_call(functools.partial(kernel, groups, segs), out_shape=(jax.Sh...]
where the time goes in v6:
time: 31.5 us; the launch traced here: 31.2 us
  Pallas kernels  30 us (95%)
  between operations  1.29 us (4%)
    pallas_call x1, Pallas kernels, shards(): pl.pallas_call(functools.partial(kernel, groups, segs), out_shape=(jax.Sh...  27 us
    pallas_call x1, Pallas kernels, shards(): pl.pallas_call(functools.partial(finish, float(length * segs)), out_shape...  2.95 us

profile of v6, /device:TPU:0, one launch (start us, length us, event | category | flops | bytes accessed | tf_op | source)
XLA Modules:
  0.0 31.2 jit_solution(2514066233809467497)
XLA Ops:
  1.3 27.0 %shard_map.103 = (f32[16,2048]{1,0:T(8,128)}, f32[8,128]{1,0:T(8,128)}) custom-call(f32[12,256,256]{2,1,0:T(8,128)} %bitcast.4, s32[1,12]{1,0:T(1,128)} %bitcast.6, s32[1,12]{1,0:T(1,128)} %bitcast.7, s32[1,1]{1,0:T(1,128)S(6)} %copy.11.count_hbm, f32[1,2048]{1,0:T(1,128)} %bitcast.5, f32[16,2048]{1,0:T(8,128)} %basis_hbm.3, f32[16,2048]{1,0:T(8,128)} %prev_hbm.1, ...), custom_call_target="tpu_custom_call" | custom-call | tf_op jit(solution)/shard_map/pallas_call | solution.py:293
  28.3 2.9 %shard_map.104 = (f32[16,2048]{1,0:T(8,128)}, f32[16,16]{1,0:T(8,128)}, f32[16,16]{1,0:T(8,128)}) custom-call(f32[16,2048]{1,0:T(8,128)} %get-tuple-element.5.rest_hbm, f32[16,2048]{1,0:T(8,128)} %basis_hbm.3, f32[8,128]{1,0:T(8,128)} %get-tuple-element.6.sums_ref, f32[16,16]{1,0:T(8,128)} %beta_prev_ref.1), custom_call_target="tpu_custom_call" | custom-call | tf_op jit(solution)/shard_map/pallas_call | solution.py:338
